TPU v7x, 256 devices: a whole 4x4x8 slice. The times are simulated.
256 devices in a mesh: dp: 32 (over z_lo, x, core), tensor: 8 (over y, z_hi).
Axes of the slice: x: 4, y: 4, z: 8 (z_hi: 2, z_lo: 4; z = z_hi * 4 + z_lo), core: 2. Of those that a mesh axis runs over, the one named last changes fastest.
Arguments:
- hidden: bfloat16 [32768, 28672], P('dp', 'tensor'), may hold values from -6 to 6
- out_grad: bfloat16 [32768, 8192], P('dp', 'tensor'), may hold values from -6 to 6
- proj_in: bfloat16 [28672, 64], P('tensor'), may hold values from -0.03125 to 0.03125
- proj_out: bfloat16 [8192, 64], P('tensor'), may hold values from -0.0625 to 0.0625
- owner_ids: int32 [32768, 1], P('dp'), may hold values from 0 to 31; in each aligned block of 1024 rows (0 to 1023, 1024 to 2047, ...) at most 128 rows name the same one
- example_ids: int32 [32768], P('dp'), may hold values from 0 to 127
Outputs:
- kernel: float32 [4096, 4096], P('tensor', 'dp')
Inputs may be any that keep to these rules, and one draw needn't show every extreme that they name: `owner_ids`: among the rows of one index of dp, at most 128 name the same owner, and every draw reaches 128.
All inputs are finite; a program needn't handle non-finite values.
Results may differ from a plain program's by a relative error of at most 0.009.
Values may be sent and summed in bfloat16 or wider, within the bound.
A program may use at most 64 MiB of HBM per device.

v0:
```python
import jax
import jax.numpy as jnp
from jax import lax
from jax.sharding import PartitionSpec as P

EX_DEV = 128


def outer_rows(x_rows, g_rows):
    return (x_rows[:, :, None] * g_rows[:, None, :]).reshape(
        x_rows.shape[0], x_rows.shape[1] * g_rows.shape[1]
    )


def member_dot(member, outer):
    member_half = member.astype(jnp.bfloat16)
    upper = outer.astype(jnp.bfloat16)
    lower = (outer - upper.astype(jnp.float32)).astype(jnp.bfloat16)
    first = jnp.dot(member_half, upper, preferred_element_type=jnp.float32)
    return first + jnp.dot(member_half, lower, preferred_element_type=jnp.float32)


def body(hidden, out_grad, proj_in, proj_out, owner_ids, example_ids):
    tensors = lax.axis_size("tensor")
    trank = lax.axis_index("tensor")
    groups = lax.axis_size("dp")
    width = proj_in.shape[1]
    share = width // tensors
    tok = hidden.shape[0]
    x_part = jnp.dot(hidden, proj_in, preferred_element_type=jnp.float32)
    g_part = jnp.dot(out_grad, proj_out, preferred_element_type=jnp.float32)
    send_rows = lax.psum(jnp.concatenate([x_part, g_part], 1), "tensor")
    x_start = trank * share
    columns = send_rows.shape[1]
    owners = owner_ids[:, 0]
    capacity = 4 * tok // groups
    owner_hot = (owners[:, None] == jnp.arange(groups, dtype=jnp.int32)[None, :]).astype(jnp.int32)
    slot_index = jnp.sum(jnp.cumsum(owner_hot, 0) * owner_hot, 1) - 1
    target = owners * capacity + slot_index
    row_buffer = jnp.zeros((groups * capacity, columns), jnp.float32).at[target].set(send_rows)
    id_buffer = (
        jnp.full((groups * capacity,), -1.0, jnp.float32)
        .at[target]
        .set(example_ids.astype(jnp.float32))
    )
    got_rows, got_ids = (
        lax.all_to_all(
            row_buffer.reshape(groups, capacity, columns),
            "dp",
            split_axis=0,
            concat_axis=0,
            tiled=True,
        ),
        lax.all_to_all(
            id_buffer.reshape(groups, capacity), "dp", split_axis=0, concat_axis=0, tiled=True
        ),
    )
    rows = got_rows.reshape(groups * capacity, columns)
    x_rows = lax.dynamic_slice_in_dim(rows, x_start, share, 1)
    g_rows = rows[:, columns - width :]
    member = (
        got_ids.reshape(1, groups * capacity) == jnp.arange(EX_DEV, dtype=jnp.float32)[:, None]
    ).astype(jnp.float32)
    sums = member_dot(member, outer_rows(x_rows, g_rows))
    counts = jnp.sum(member, 1)
    grads = (sums / jnp.maximum(counts, 1.0)[:, None]).astype(jnp.bfloat16)
    products = (
        lax.dot_general(
            lax.all_gather(grads, "dp", axis=0, tiled=True),
            grads,
            (((1,), (1,)), ((), ())),
            preferred_element_type=jnp.float32,
        )
        / width
    )
    return lax.psum_scatter(products, "tensor", scatter_dimension=0, tiled=True)


def solution(mesh):
    in_specs = (
        P("dp", "tensor"),
        P("dp", "tensor"),
        P("tensor", None),
        P("tensor", None),
        P("dp", None),
        P("dp"),
    )
    out_specs = P("tensor", "dp")
    return jax.shard_map(body, mesh=mesh, in_specs=in_specs, out_specs=out_specs, check_vma=False)
```

profile of v0, /device:TPU:6, one launch (start us, length us, event | category | flops | bytes accessed | tf_op | source)
XLA Modules:
  0.0 376.6 jit_solution(12380154530716794183)
XLA Ops:
  6.5 5.6 %fusion.15 = f32[1024,64]{0,1:T(8,128)S(1)} fusion(bf16[1024,3584]{1,0:T(8,128)(2,1)} %param.6, bf16[3584,64]{0,1:T(8,128)(2,1)} %param.8), kind=kOutput, calls=%fused_computation.33 | convolution fusion | flops 469762048 | bytes 8060928 | tf_op jit(solution)/shard_map/dot_general | solution.py:30
  12.2 0.8 fusion.16
  12.9 0.9 pad_maximum_fusion
  13.8 9.0 %reduce-window.6 = s32[32,8,128]{2,1,0:T(8,128)S(1)} reduce-window(s32[32,8,128]{2,1,0:T(8,128)S(1)} %fusion.12, s32[]{:T(128)} %constant.12.clone.1), window={size=1x1x128 pad=0_0x0_0x127_0}, to_apply=%region_0.0 | reduce-window | flops 4161536 | bytes 262148 | tf_op jit(solution)/shard_map/reduce-window
  22.9 0.1 copy.12
  23.4 4.9 %scatter_custom_fusion = f32[4096]{0:T(1024)} fusion(s32[1024]{0:T(1024)S(1)} %bitcast.45, f32[1024]{0:T(1024)S(1)} %convert_element_type.27, f32[]{:T(128)} %constant.10.clone.1), kind=kCustom, calls=%fused_computation.28 | custom fusion | bytes 16388 | tf_op jit(solution)/shard_map/scatter | solution.py:44
  28.3 9.0 %all-to-all-start = ((f32[32,1,128]{2,1,0:T(1,128)}), f32[32,1,128]{2,1,0:T(1,128)S(1)}, u32[]{:S(2)}, u32[]{:S(2)}) async-start(f32[32,1,128]{2,1,0:T(1,128)} %bitcast.6), calls=%async_computation | async-start | bytes 32768 | tf_op jit(solution)/shard_map/all_to_all | solution.py:54
  37.3 91.8 %all-reduce.2.cloned.1.call-done = f32[1024,128]{0,1:T(8,128)} async-done(((f32[1024,128]{0,1:T(8,128)}), f32[1024,128]{0,1:T(8,128)}) %all-reduce.2.cloned.1.call-update) | async-done | bytes 524304 | tf_op jit(solution)/shard_map/psum | solution.py:32
  129.1 1.2 copy.14
  130.3 4.5 %scatter_custom_fusion.1 = f32[4096,128]{1,0:T(8,128)} fusion(s32[1024]{0:T(1024)S(1)} %bitcast.46, f32[1024,128]{1,0:T(8,128)S(1)} %copy.14, f32[]{:T(128)} %constant.6.clone.1), kind=kCustom, calls=%fused_computation.15 | custom fusion | bytes 2097156 | tf_op jit(solution)/shard_map/scatter | solution.py:40
  134.8 5.0 %all-to-all-start.1 = ((f32[32,128,128]{2,1,0:T(8,128)}), f32[32,128,128]{2,1,0:T(8,128)}, u32[]{:S(2)}, u32[]{:S(2)}) async-start(f32[32,128,128]{2,1,0:T(8,128)} %bitcast.36), calls=%async_computation.1 | async-start | bytes 4194304 | tf_op jit(solution)/shard_map/all_to_all | solution.py:47
  139.8 0.3 convert_reduce_fusion
  140.1 48.2 %all-to-all-done.1 = f32[32,128,128]{2,1,0:T(8,128)} async-done(((f32[32,128,128]{2,1,0:T(8,128)}), f32[32,128,128]{2,1,0:T(8,128)}, u32[]{:S(2)}, u32[]{:S(2)}) %all-to-all-start.1) | async-done | bytes 2097184 | tf_op jit(solution)/shard_map/all_to_all | solution.py:47
  188.3 3.5 slice.14
  191.8 3.5 constant_dynamic-slice_fusion
  195.3 2.2 copy.17
  197.5 2.2 copy.18
  199.7 1.0 broadcast_multiply_fusion
  200.7 4.7 %fusion = (bf16[4096,512]{0,1:T(8,128)(2,1)}, bf16[4096,512]{0,1:T(8,128)(2,1)}) fusion(f32[4096,8,64]{0,2,1:T(8,128)S(1)} %broadcast_multiply_fusion), kind=kLoop, calls=%fused_computation.4 | loop fusion | flops 8388608 | bytes 16777216 | tf_op jit(solution)/shard_map/convert_element_type | solution.py:18
  205.4 3.8 %fusion.1 = f32[128,512]{1,0:T(8,128)S(1)} fusion(bf16[4096,512]{0,1:T(8,128)(2,1)} %get-tuple-element.5, f32[4096]{0:T(1024)S(1)} %bitcast.39), kind=kOutput, calls=%fused_computation.10 | convolution fusion | flops 538443776 | bytes 4472832 | tf_op jit(solution)/shard_map/dot_general | solution.py:20
  209.3 2.2 fusion.5
  211.5 58.5 %all-gather.2.cloned.1.call-done = bf16[4096,512]{1,0:T(8,128)(2,1)} async-done(((bf16[128,512]{1,0:T(8,128)(2,1)}), bf16[4096,512]{1,0:T(8,128)(2,1)}) %all-gather.2.cloned.1.call-update) | async-done | bytes 4194320 | tf_op jit(solution)/shard_map/all_gather | solution.py:69
  270.1 4.8 %convolution_multiply_fusion = f32[4096,128]{1,0:T(8,128)} fusion(bf16[4096,512]{1,0:T(8,128)(2,1)} %all-gather.2.cloned.1.call-done, bf16[128,512]{1,0:T(8,128)(2,1)} %fusion.5), kind=kOutput, calls=%fused_computation.5 | convolution fusion | flops 537395200 | bytes 6422528 | tf_op jit(solution)/shard_map/dot_general | solution.py:68
  274.9 95.2 %reduce-scatter.2.cloned.1.call-done = f32[512,128]{1,0:T(8,128)} async-done(((f32[4096,128]{1,0:T(8,128)}), f32[512,128]{1,0:T(8,128)}) %reduce-scatter.2.cloned.1.call-update) | async-done | bytes 262160 | tf_op jit(solution)/shard_map/reduce_scatter | solution.py:76
  (28 shorter events, 0.5 us)
Async XLA Ops:
  6.5 5.6 %copy-start = (bf16[1024,1024]{1,0:T(8,128)(2,1)S(1)}, bf16[1024,1024]{1,0:T(8,128)(2,1)}, u32[]{:S(2)}) copy-start(bf16[1024,1024]{1,0:T(8,128)(2,1)} %param.7) | copy-start | bytes 6291460
  6.5 5.6 %copy-start.2 = (bf16[1024,64]{0,1:T(8,128)(2,1)S(1)}, bf16[1024,64]{0,1:T(8,128)(2,1)}, u32[]{:S(2)}) copy-start(bf16[1024,64]{0,1:T(8,128)(2,1)} %param.9) | copy-start | bytes 393220
  6.5 122.5 %all-reduce.2.cloned.1.call-start = ((), (), s32[]{:S(2)}) async-start(), calls=%async_computation.3 | async-start | bytes 1048576 | tf_op jit(solution)/shard_map/psum | solution.py:32
  12.1 1.7 copy-start.3
  12.1 11.2 %copy-start.4 = (s32[1024]{0:T(1024)S(1)}, s32[1024]{0:T(1024)}, u32[]{:S(2)}) copy-start(s32[1024]{0:T(1024)} %param.11) | copy-start | bytes 12292
  28.3 106.5 %all-to-all-start = ((f32[32,1,128]{2,1,0:T(1,128)}), f32[32,1,128]{2,1,0:T(1,128)S(1)}, u32[]{:S(2)}, u32[]{:S(2)}) async-start(f32[32,1,128]{2,1,0:T(1,128)} %bitcast.6), calls=%async_computation | async-start | bytes 32768 | tf_op jit(solution)/shard_map/all_to_all | solution.py:54
  134.8 53.5 %all-to-all-start.1 = ((f32[32,128,128]{2,1,0:T(8,128)}), f32[32,128,128]{2,1,0:T(8,128)}, u32[]{:S(2)}, u32[]{:S(2)}) async-start(f32[32,128,128]{2,1,0:T(8,128)} %bitcast.36), calls=%async_computation.1 | async-start | bytes 4194304 | tf_op jit(solution)/shard_map/all_to_all | solution.py:47
  139.8 130.3 %all-gather.2.cloned.1.call-start = ((), (), s32[]{:S(2)}) async-start(), calls=%async_computation.4 | async-start | bytes 4325376 | tf_op jit(solution)/shard_map/all_gather | solution.py:69
  205.4 3.9 %copy-start.1 = (bf16[4096,512]{0,1:T(8,128)(2,1)S(1)}, bf16[4096,512]{0,1:T(8,128)(2,1)}, u32[]{:S(2)}) copy-start(bf16[4096,512]{0,1:T(8,128)(2,1)} %get-tuple-element.6) | copy-start | bytes 12582916
  211.5 158.6 %reduce-scatter.2.cloned.1.call-start = ((), (), s32[]{:S(2)}) async-start(), calls=%async_computation.5 | async-start | bytes 2359296 | tf_op jit(solution)/shard_map/reduce_scatter | solution.py:76
Sparse Core Ops, SparseCore 0:
  13.9 115.0 all-reduce.1
  211.6 58.4 all-gather.1
  275.0 95.0 reduce-scatter.1
where the time goes:
time: 377 us
  waiting for transfers between devices  294 us (78%)
  local copies, waits for them, and re-layouts  22.3 us (6%)
  matrix products  17.1 us (5%)
  other arithmetic  16.1 us (4%)
  starting transfers between devices  14.1 us (4%)
  between operations  13.3 us (4%)
    reduce_scatter x1, waiting for transfers between devices, body(): return lax.psum_scatter(products, 'tensor', scatter_dimension=0, tiled=True)  95.2 us
    psum x1, waiting for transfers between devices, body(): send_rows = lax.psum(jnp.concatenate([x_part, g_part], 1), 'tensor')  91.8 us
    all_gather x1, waiting for transfers between devices, body(): lax.all_gather(grads, 'dp', axis=0, tiled=True)  58.5 us
    all_to_all x1, waiting for transfers between devices, body(): lax.all_to_all(row_buffer.reshape(groups, capacity, columns), 'dp', split...  48.2 us
    another operation x3, other arithmetic  9.15 us
    all_to_all x1, starting transfers between devices, body(): lax.all_to_all(id_buffer.reshape(groups, capacity), 'dp', split_axis=0, c...  8.99 us
  transfers between devices with their start and end apart: 5, of which 4 were waited for; matrix products, arithmetic and copies ran while one was open for 5% of the time, Pallas kernels for 0%

commit v1 on v0

--- a/solution.py
+++ b/solution.py
@@ -66,7 +66,9 @@
     grads = (sums / jnp.maximum(counts, 1.0)[:, None]).astype(jnp.bfloat16)
     products = (
         lax.dot_general(
-            lax.all_gather(grads, "dp", axis=0, tiled=True),
+            jnp.concatenate(
+                lax.all_to_all(jnp.stack([grads] * lax.axis_size("dp")), "dp", 0, 0), axis=0
+            ),
             grads,
             (((1,), (1,)), ((), ())),
             preferred_element_type=jnp.float32,

time: 377 us -> 413 us (1.095)
  blocking collectives: 0 us -> 99.2 us
  waiting for transfers between devices: 294 us -> 232 us
    all_to_all x0 -> x1, blocking collectives: none -> 99.2 us  [body(): lax.all_to_all(jnp.stack([grads] * lax.axis_size('dp')), 'dp', 0, 0)]
    all_gather x1 -> x0, waiting for transfers between devices: 58.5 us -> none  [body(): lax.all_gather(grads, 'dp', axis=0, tiled=True)]
  transfers between devices with their start and end apart: 5 -> 4, of which waited for: 4 -> 3; matrix products, arithmetic and copies ran while one was open for 5% -> 5% of each run, Pallas kernels for 0% -> 0%
where the time goes in v1:
time: 413 us; the launch traced here: 412 us
  waiting for transfers between devices  232 us (56%)
  blocking collectives  99.2 us (24%)
  local copies, waits for them, and re-layouts  22.7 us (5%)
  other arithmetic  16.1 us (4%)
  matrix products  14.3 us (3%)
  starting transfers between devices  14 us (3%)
  between operations  13.6 us (3%)
    all_to_all x1, blocking collectives, body(): lax.all_to_all(jnp.stack([grads] * lax.axis_size('dp')), 'dp', 0, 0)  99.2 us
    reduce_scatter x1, waiting for transfers between devices, body(): return lax.psum_scatter(products, 'tensor', scatter_dimension=0, tiled=True)  92.3 us
    psum x1, waiting for transfers between devices, body(): send_rows = lax.psum(jnp.concatenate([x_part, g_part], 1), 'tensor')  91.8 us
    all_to_all x1, waiting for transfers between devices, body(): lax.all_to_all(row_buffer.reshape(groups, capacity, columns), 'dp', split...  48.2 us
    another operation x3, other arithmetic  9.15 us
    all_to_all x1, starting transfers between devices, body(): lax.all_to_all(id_buffer.reshape(groups, capacity), 'dp', split_axis=0, c...  8.99 us
  transfers between devices with their start and end apart: 4, of which 3 were waited for; matrix products, arithmetic and copies ran while one was open for 5% of the time, Pallas kernels for 0%

profile of v1, /device:TPU:6, one launch (start us, length us, event | category | flops | bytes accessed | tf_op | source)
XLA Modules:
  0.0 412.3 jit_solution(7781213369539019331)
XLA Ops:
  6.5 5.6 %fusion.15 = f32[1024,64]{0,1:T(8,128)S(1)} fusion(bf16[1024,3584]{1,0:T(8,128)(2,1)} %param.6, bf16[3584,64]{0,1:T(8,128)(2,1)} %param.8), kind=kOutput, calls=%fused_computation.33 | convolution fusion | flops 469762048 | bytes 8060928 | tf_op jit(solution)/shard_map/dot_general | solution.py:30
  12.2 0.8 fusion.16
  12.9 0.9 pad_maximum_fusion
  13.8 9.0 %reduce-window.6 = s32[32,8,128]{2,1,0:T(8,128)S(1)} reduce-window(s32[32,8,128]{2,1,0:T(8,128)S(1)} %fusion.12, s32[]{:T(128)} %constant.12.clone.1), window={size=1x1x128 pad=0_0x0_0x127_0}, to_apply=%region_0.0 | reduce-window | flops 4161536 | bytes 262148 | tf_op jit(solution)/shard_map/reduce-window
  23.4 4.9 %scatter_custom_fusion = f32[4096]{0:T(1024)} fusion(s32[1024]{0:T(1024)S(1)} %bitcast.47, f32[1024]{0:T(1024)S(1)} %convert_element_type.27, f32[]{:T(128)} %constant.10.clone.1), kind=kCustom, calls=%fused_computation.28 | custom fusion | bytes 16388 | tf_op jit(solution)/shard_map/scatter | solution.py:44
  28.3 9.0 %all-to-all-start = ((f32[32,1,128]{2,1,0:T(1,128)}), f32[32,1,128]{2,1,0:T(1,128)S(1)}, u32[]{:S(2)}, u32[]{:S(2)}) async-start(f32[32,1,128]{2,1,0:T(1,128)} %bitcast.6), calls=%async_computation | async-start | bytes 32768 | tf_op jit(solution)/shard_map/all_to_all | solution.py:54
  37.3 91.8 %all-reduce.2.cloned.1.call-done = f32[1024,128]{0,1:T(8,128)} async-done(((f32[1024,128]{0,1:T(8,128)}), f32[1024,128]{0,1:T(8,128)}) %all-reduce.2.cloned.1.call-update) | async-done | bytes 524304 | tf_op jit(solution)/shard_map/psum | solution.py:32
  129.1 1.2 copy.14
  130.3 4.5 %scatter_custom_fusion.1 = f32[4096,128]{1,0:T(8,128)} fusion(s32[1024]{0:T(1024)S(1)} %bitcast.48, f32[1024,128]{1,0:T(8,128)S(1)} %copy.14, f32[]{:T(128)} %constant.6.clone.1), kind=kCustom, calls=%fused_computation.15 | custom fusion | bytes 2097156 | tf_op jit(solution)/shard_map/scatter | solution.py:40
  134.8 5.0 %all-to-all-start.1 = ((f32[32,128,128]{2,1,0:T(8,128)}), f32[32,128,128]{2,1,0:T(8,128)}, u32[]{:S(2)}, u32[]{:S(2)}) async-start(f32[32,128,128]{2,1,0:T(8,128)} %bitcast.38), calls=%async_computation.1 | async-start | bytes 4194304 | tf_op jit(solution)/shard_map/all_to_all | solution.py:47
  139.8 0.3 convert_reduce_fusion
  140.1 48.2 %all-to-all-done.1 = f32[32,128,128]{2,1,0:T(8,128)} async-done(((f32[32,128,128]{2,1,0:T(8,128)}), f32[32,128,128]{2,1,0:T(8,128)}, u32[]{:S(2)}, u32[]{:S(2)}) %all-to-all-start.1) | async-done | bytes 2097184 | tf_op jit(solution)/shard_map/all_to_all | solution.py:47
  188.3 3.5 slice.14
  191.8 3.5 constant_dynamic-slice_fusion
  195.3 2.2 copy.17
  197.5 2.2 copy.18
  199.7 1.0 broadcast_multiply_fusion
  200.7 4.7 %fusion = (bf16[4096,512]{0,1:T(8,128)(2,1)}, bf16[4096,512]{0,1:T(8,128)(2,1)}) fusion(f32[4096,8,64]{0,2,1:T(8,128)S(1)} %broadcast_multiply_fusion), kind=kLoop, calls=%fused_computation.4 | loop fusion | flops 8388608 | bytes 16777216 | tf_op jit(solution)/shard_map/convert_element_type | solution.py:18
  205.4 3.8 fusion.1
  209.3 1.5 fusion.5
  210.8 0.5 stack.2
  211.3 99.2 %all_to_all.19 = bf16[32,128,512]{2,1,0:T(8,128)(2,1)S(1)} all-to-all(bf16[32,128,512]{2,1,0:T(8,128)(2,1)S(1)} %stack.2), channel_id=1, replica_groups=mesh['dp'=32,'tensor'=8] {'dp'}, dimensions={0} | all-to-all | bytes 8388608 | tf_op jit(solution)/shard_map/all_to_all | solution.py:70
  310.5 2.6 convolution_multiply_fusion
  313.1 92.3 %reduce-scatter.2.cloned.1.call-done = f32[512,128]{1,0:T(8,128)} async-done(((f32[4096,128]{1,0:T(8,128)}), f32[512,128]{1,0:T(8,128)}) %reduce-scatter.2.cloned.1.call-update) | async-done | bytes 262160 | tf_op jit(solution)/shard_map/reduce_scatter | solution.py:78
  (27 shorter events, 0.6 us)
Async XLA Ops:
  6.5 5.6 %copy-start = (bf16[1024,1024]{1,0:T(8,128)(2,1)S(1)}, bf16[1024,1024]{1,0:T(8,128)(2,1)}, u32[]{:S(2)}) copy-start(bf16[1024,1024]{1,0:T(8,128)(2,1)} %param.7) | copy-start | bytes 6291460
  6.5 5.6 %copy-start.2 = (bf16[1024,64]{0,1:T(8,128)(2,1)S(1)}, bf16[1024,64]{0,1:T(8,128)(2,1)}, u32[]{:S(2)}) copy-start(bf16[1024,64]{0,1:T(8,128)(2,1)} %param.9) | copy-start | bytes 393220
  6.5 122.5 %all-reduce.2.cloned.1.call-start = ((), (), s32[]{:S(2)}) async-start(), calls=%async_computation.4 | async-start | bytes 1048576 | tf_op jit(solution)/shard_map/psum | solution.py:32
  12.1 1.7 copy-start.3
  12.1 11.2 %copy-start.4 = (s32[1024]{0:T(1024)S(1)}, s32[1024]{0:T(1024)}, u32[]{:S(2)}) copy-start(s32[1024]{0:T(1024)} %param.11) | copy-start | bytes 12292
  28.3 106.5 %all-to-all-start = ((f32[32,1,128]{2,1,0:T(1,128)}), f32[32,1,128]{2,1,0:T(1,128)S(1)}, u32[]{:S(2)}, u32[]{:S(2)}) async-start(f32[32,1,128]{2,1,0:T(1,128)} %bitcast.6), calls=%async_computation | async-start | bytes 32768 | tf_op jit(solution)/shard_map/all_to_all | solution.py:54
  134.8 53.5 %all-to-all-start.1 = ((f32[32,128,128]{2,1,0:T(8,128)}), f32[32,128,128]{2,1,0:T(8,128)}, u32[]{:S(2)}, u32[]{:S(2)}) async-start(f32[32,128,128]{2,1,0:T(8,128)} %bitcast.38), calls=%async_computation.1 | async-start | bytes 4194304 | tf_op jit(solution)/shard_map/all_to_all | solution.py:47
  139.8 265.6 %reduce-scatter.2.cloned.1.call-start = ((), (), s32[]{:S(2)}) async-start(), calls=%async_computation.5 | async-start | bytes 2359296 | tf_op jit(solution)/shard_map/reduce_scatter | solution.py:78
  205.4 3.9 copy-start.1
Sparse Core Ops, SparseCore 0:
  13.9 115.0 all-reduce.1
  313.2 92.1 reduce-scatter.1
